TPU v7x, 512 devices: a whole 4x4x16 slice. The times are simulated.
512 devices in a mesh: ad: 64 (over z, x), tp: 8 (over y, core).
Axes of the slice: x: 4, y: 4, z: 16, core: 2. Of those that a mesh axis runs over, the one named last changes fastest.
Arguments:
- tokens: bfloat16 [4, 3072, 8192], P(None, 'ad', 'tp'), may hold values from -6 to 6
- row_adapter_index: int32 [4, 3072], P(None, 'ad'), may hold values from 0 to 255, as said below
- key_base_weight: bfloat16 [8192, 1024], P('tp'), may hold values from -0.0625 to 0.0625
- adapter_down_weight: bfloat16 [256, 8192, 64], P('ad', 'tp'), may hold values from -0.0625 to 0.0625
- adapter_up_weight: bfloat16 [256, 64, 1024], P('ad', None, 'tp'), may hold values from -0.75 to 0.75
Outputs:
- token_keys_output: bfloat16 [4, 3072, 1024], P(None, 'ad', 'tp')
Inputs may be any that keep to these rules, and one draw needn't show every extreme that they name: `row_adapter_index`: group g holds adapters g * 4 to (g + 1) * 4 - 1. In each step the 48 rows of one index of ad name one group in exactly 2 rows and every other group in at most 1 row; that busiest group is the same for every index of ad in a step, so it receives 2 rows from each.
All inputs are finite; a program needn't handle non-finite values.
Results may differ from a plain program's by a relative error of at most 0.005.
Values may be sent and summed in bfloat16 or wider, within the bound.
A program may use at most 64 MiB of HBM per device.

v0:
```python
import jax
import jax.numpy as jnp
from jax import lax
from jax.sharding import PartitionSpec as P

TAG_WIDTH = 128


def body(tokens, row_adapter_index, key_base_weight, adapter_down_weight, adapter_up_weight):
    step_count, row_dev, width_per_shard = tokens.shape
    groups = lax.axis_size("ad")
    me = lax.axis_index("ad")
    adapter_number = adapter_down_weight.shape[0]
    rank = adapter_down_weight.shape[2]
    row_total = step_count * row_dev
    regular_total = groups * step_count
    wide = width_per_shard + TAG_WIDTH
    gathered_rows = tokens.reshape(row_total, width_per_shard)
    index_list = row_adapter_index.reshape(step_count, row_dev)
    owner_group = index_list // adapter_number
    local_index = index_list % adapter_number
    group_hits = (
        owner_group[:, :, None] == jnp.arange(groups, dtype=jnp.int32)[None, None, :]
    ).astype(jnp.int32)
    slot_rank = jnp.sum((jnp.cumsum(group_hits, axis=1) - group_hits) * group_hits, axis=2)
    step_ids = jnp.arange(step_count, dtype=jnp.int32)[:, None]
    first = slot_rank == 0
    regular_slot = jnp.where(first, owner_group * step_count + step_ids, -1).reshape(row_total)
    overflow_slot = jnp.where(slot_rank == 1, step_ids, -1).reshape(row_total)
    dispatch = (
        regular_slot[None, :] == jnp.arange(regular_total, dtype=jnp.int32)[:, None]
    ).astype(jnp.bfloat16)
    dispatch_over = (
        overflow_slot[None, :] == jnp.arange(step_count, dtype=jnp.int32)[:, None]
    ).astype(jnp.bfloat16)
    tag_values = jnp.where(first, local_index + 1, index_list + 1).astype(jnp.bfloat16)
    tag_block = jnp.broadcast_to(tag_values.reshape(row_total, 1), (row_total, TAG_WIDTH))
    rows_tagged = jnp.concatenate([gathered_rows, tag_block], axis=1)
    send_rows = jnp.dot(dispatch, rows_tagged, preferred_element_type=jnp.float32).astype(
        jnp.bfloat16
    )
    send_rows = send_rows.reshape(groups, step_count, wide)
    send_over = jnp.dot(dispatch_over, rows_tagged, preferred_element_type=jnp.float32).astype(
        jnp.bfloat16
    )
    incoming_over = lax.all_gather(send_over, "ad", tiled=True)
    incoming = lax.all_to_all(send_rows, "ad", split_axis=0, concat_axis=0, tiled=True)
    partial_base = jnp.dot(gathered_rows, key_base_weight, preferred_element_type=jnp.float32)
    partial_base, incoming_over = lax.optimization_barrier((partial_base, incoming_over))
    base_keys_output = lax.psum_scatter(partial_base, "tp", scatter_dimension=1, tiled=True)
    key_feature_width = base_keys_output.shape[1]
    incoming = jnp.concatenate([incoming.reshape(regular_total, wide), incoming_over], axis=0)
    slot_total = incoming.shape[0]
    incoming_rows = incoming[:, :width_per_shard]
    regular_labels = incoming[:regular_total, width_per_shard].astype(jnp.float32)
    over_labels = incoming[regular_total:, width_per_shard].astype(jnp.float32) - (
        me * adapter_number
    ).astype(jnp.float32)
    incoming_labels = jnp.concatenate([regular_labels, over_labels])
    down_all = jnp.einsum(
        "nd,adr->nar", incoming_rows, adapter_down_weight, preferred_element_type=jnp.float32
    )
    labels = (jnp.arange(adapter_number, dtype=jnp.int32) + 1).astype(jnp.float32)
    selector = (incoming_labels[:, None] == labels[None, :]).astype(jnp.float32)
    down_part = jnp.sum(down_all * selector[:, :, None], axis=1)
    down_sum = lax.psum(down_part, "tp")
    down_low = down_sum.astype(jnp.bfloat16)
    spread_rows = (selector.astype(jnp.bfloat16)[:, :, None] * down_low[:, None, :]).reshape(
        slot_total, adapter_number * rank
    )
    up_flat = adapter_up_weight.reshape(adapter_number * rank, key_feature_width)
    adapter_update = jnp.dot(spread_rows, up_flat, preferred_element_type=jnp.float32).astype(
        jnp.bfloat16
    )
    update_regular = adapter_update[:regular_total].reshape(groups, step_count, key_feature_width)
    update_over = adapter_update[regular_total:].reshape(groups, step_count, key_feature_width)
    send_back = jnp.concatenate([update_regular, update_over], axis=1)
    rows_sent_back = lax.all_to_all(send_back, "ad", split_axis=0, concat_axis=0, tiled=True)
    back_regular = rows_sent_back[:, :step_count].reshape(regular_total, key_feature_width)
    back_over = jnp.sum(rows_sent_back[:, step_count:].astype(jnp.float32), axis=0)
    routed = jnp.dot(dispatch.T, back_regular, preferred_element_type=jnp.float32) + jnp.dot(
        dispatch_over.T.astype(jnp.float32), back_over, preferred_element_type=jnp.float32
    )
    out = (base_keys_output + routed).astype(jnp.bfloat16)
    return out.reshape(step_count, row_dev, key_feature_width)


def solution(mesh):
    placed = (
        P(None, "ad", "tp"),
        P(None, "ad"),
        P("tp", None),
        P("ad", "tp", None),
        P("ad", None, "tp"),
    )
    return jax.shard_map(
        body, mesh=mesh, in_specs=placed, out_specs=P(None, "ad", "tp"), check_vma=False
    )
```

profile of v0, /device:TPU:2, one launch (start us, length us, event | category | flops | bytes accessed | tf_op | source)
XLA Modules:
  0.0 221.5 jit_solution(2728375814923560662)
XLA Ops:
  6.5 0.0 copy-start
  6.5 0.0 copy-start.2
  6.5 0.8 add_select_fusion.1
  7.4 0.1 fusion.11
  7.5 0.1 reduce_window_sum.11
  7.6 0.2 select_reduce_fusion
  7.8 0.7 add_select_fusion.2
  8.5 0.7 fusion.15
  9.2 0.1 broadcast_in_dim.19
  9.3 0.1 eq.83
  9.4 0.1 broadcast_in_dim.20
  9.5 1.3 convolution_convert_fusion
  10.8 1.0 reshape.110
  11.8 18.6 %all-to-all-start = ((bf16[64,4,1152]{2,1,0:T(4,128)(2,1)}), bf16[64,4,1152]{2,1,0:T(4,128)(2,1)S(1)}, u32[]{:S(2)}, u32[]{:S(2)}) async-start(bf16[64,4,1152]{2,1,0:T(4,128)(2,1)} %reshape.110), calls=%async_computation.1 | async-start | bytes 1179648 | tf_op jit(solution)/shard_map/all_to_all | solution.py:47
  30.4 0.0 reduce-scatter.2.cloned.1.call-start
  30.5 0.1 select_n.32
  30.6 0.0 copy-done.2
  30.6 0.2 fusion
  30.7 120.6 %all-gather = bf16[64,4,1152]{2,1,0:T(4,128)(2,1)S(1)} all-gather(bf16[1,4,1152]{2,1,0:T(4,128)(2,1)S(1)} %fusion), channel_id=1, replica_groups=mesh['ad'=64,'tp'=8] {'ad'}, dimensions={0}, use_global_device_ids=true | all-gather | bytes 599040 | tf_op jit(solution)/shard_map/all_gather | solution.py:46
  151.3 1.0 reshape.118
  152.3 0.0 copy-done
  152.3 0.0 copy-start.1
  152.3 2.5 %fusion.25 = f32[192,1024]{1,0:T(8,128)} fusion(bf16[192,1024]{1,0:T(8,128)(2,1)} %bitcast.23, bf16[1024,1024]{1,0:T(8,128)(2,1)S(1)} %copy-done), kind=kOutput, calls=%fused_computation.52 | convolution fusion | flops 402653184 | bytes 3276800 | tf_op jit(solution)/shard_map/dot_general | solution.py:48
  154.8 0.0 reduce-scatter.2.cloned.1.call-update
  154.9 0.0 copy-done.1
  154.9 0.1 subtract_reduce_fusion
  155.0 0.0 all-to-all-done
  155.0 1.0 reshape.111
  156.0 0.0 copy-start.3
  156.0 1.0 convert_reduce_fusion
  156.9 1.7 fusion.4
  158.7 0.1 fusion.23
  158.7 0.1 multiply_reduce_fusion
  158.8 24.9 %all-reduce.1 = bf16[512,64]{0,1:T(8,128)(2,1)S(1)} all-reduce(f32[512,64]{0,1:T(8,128)S(1)} %multiply_reduce_fusion), channel_id=1, replica_groups=mesh['ad'=64,'tp'=8] {'tp'}, use_global_device_ids=true, to_apply=%region_4.5 | all-reduce | flops 32768 | bytes 196608 | tf_op jit(solution)/shard_map/psum | solution.py:66
  183.7 0.0 copy-done.3
  183.7 0.3 fusion.1
  184.0 0.1 pad_maximum_fusion.5
  184.0 28.5 %all_to_all.10 = bf16[64,8,128]{2,1,0:T(8,128)(2,1)S(1)} all-to-all(bf16[64,8,128]{2,1,0:T(8,128)(2,1)S(1)} %pad_maximum_fusion.5), channel_id=1, replica_groups=mesh['ad'=64,'tp'=8] {'ad'}, dimensions={0} | all-to-all | bytes 262144 | tf_op jit(solution)/shard_map/all_to_all | solution.py:78
  212.6 0.1 convert_reduce_fusion.1
  212.6 0.2 fusion.12
  212.9 0.0 reduce-scatter.2.cloned.1.call-done
  212.9 1.8 fusion.3
  (4 shorter events, 0.0 us)
Async XLA Ops:
  6.5 145.8 %copy-start = (bf16[1024,1024]{1,0:T(8,128)(2,1)S(1)}, bf16[1024,1024]{1,0:T(8,128)(2,1)}, u32[]{:S(2)}) copy-start(bf16[1024,1024]{1,0:T(8,128)(2,1)} %param.7) | copy-start | bytes 6291460
  6.5 24.0 %copy-start.2 = (bf16[4,48,1024]{2,1,0:T(8,128)(2,1)S(1)}, bf16[4,48,1024]{2,1,0:T(8,128)(2,1)}, u32[]{:S(2)}) copy-start(bf16[4,48,1024]{2,1,0:T(8,128)(2,1)} %param.5) | copy-start | bytes 1179652
  11.8 143.2 %all-to-all-start = ((bf16[64,4,1152]{2,1,0:T(4,128)(2,1)}), bf16[64,4,1152]{2,1,0:T(4,128)(2,1)S(1)}, u32[]{:S(2)}, u32[]{:S(2)}) async-start(bf16[64,4,1152]{2,1,0:T(4,128)(2,1)} %reshape.110), calls=%async_computation.1 | async-start | bytes 1179648 | tf_op jit(solution)/shard_map/all_to_all | solution.py:47
  30.4 182.5 %reduce-scatter.2.cloned.1.call-start = ((), (), s32[]{:S(2)}) async-start(), calls=%async_computation.3 | async-start | bytes 884736 | tf_op jit(solution)/shard_map/reduce_scatter | solution.py:50
  152.3 2.6 %copy-start.1 = (bf16[256,1152]{1,0:T(8,128)(2,1)S(1)}, bf16[256,1152]{1,0:T(8,128)(2,1)}, u32[]{:S(2)}) copy-start(bf16[256,1152]{1,0:T(8,128)(2,1)} %reshape.118) | copy-start | bytes 1769476
  156.0 27.7 %copy-start.3 = (bf16[4,64,128]{2,1,0:T(8,128)(2,1)S(1)}, bf16[4,64,128]{2,1,0:T(8,128)(2,1)}, u32[]{:S(2)}) copy-start(bf16[4,64,128]{2,1,0:T(8,128)(2,1)} %param.9) | copy-start | bytes 196612
Sparse Core Ops, SparseCore 0:
  155.0 38.6 reduce-scatter.1
where the time goes:
time: 222 us; the launch traced here: 221 us
  blocking collectives  174 us (78%)
  starting transfers between devices  18.7 us (8%)
  between operations  13.5 us (6%)
  matrix products  7.98 us (4%)
  other arithmetic  4.05 us (2%)
  local copies, waits for them, and re-layouts  3.28 us (1%)
    all_gather x1, blocking collectives, body(): incoming_over = lax.all_gather(send_over, 'ad', tiled=True)  121 us
    all_to_all x1, blocking collectives, body(): lax.all_to_all(send_back, 'ad', split_axis=0, concat_axis=0, tiled=True)  28.5 us
    psum x1, blocking collectives, body(): down_sum = lax.psum(down_part, 'tp')  24.9 us
    all_to_all x1, starting transfers between devices, body(): lax.all_to_all(send_rows, 'ad', split_axis=0, concat_axis=0, tiled=True)  18.6 us
  transfers between devices with their start and end apart: 2, of which 0 were waited for; matrix products, arithmetic and copies ran while one was open for 4% of the time, Pallas kernels for 0%

commit v1 on v0

--- a/solution.py
+++ b/solution.py
@@ -63,7 +63,7 @@
     labels = (jnp.arange(adapter_number, dtype=jnp.int32) + 1).astype(jnp.float32)
     selector = (incoming_labels[:, None] == labels[None, :]).astype(jnp.float32)
     down_part = jnp.sum(down_all * selector[:, :, None], axis=1)
-    down_sum = lax.psum(down_part, "tp")
+    down_sum = jnp.sum(lax.all_gather(down_part, "tp"), axis=0)
     down_low = down_sum.astype(jnp.bfloat16)
     spread_rows = (selector.astype(jnp.bfloat16)[:, :, None] * down_low[:, None, :]).reshape(
         slot_total, adapter_number * rank

time: 222 us -> 241 us (1.086)
  waiting for transfers between devices: 0.03 us -> 37.6 us
  blocking collectives: 174 us -> 153 us
    all_gather x0 -> x1, waiting for transfers between devices: none -> 29.5 us  [body(): down_sum = jnp.sum(lax.all_gather(down_part, 'tp'), axis=0)]
    psum x1 -> x0, blocking collectives: 24.9 us -> none  [body(): down_sum = lax.psum(down_part, 'tp')]
    reduce_scatter x1, waiting for transfers between devices: 0.02 us -> 7.39 us  [body(): lax.psum_scatter(partial_base, 'tp', scatter_dimension=1, tiled=True)]
    all_to_all x1, blocking collectives: 28.5 us -> 32.5 us  [body(): lax.all_to_all(send_back, 'ad', split_axis=0, concat_axis=0, tiled=True)]
  transfers between devices with their start and end apart: 2 -> 3, of which waited for: 0 -> 2; matrix products, arithmetic and copies ran while one was open for 4% -> 3% of each run, Pallas kernels for 0% -> 0%
where the time goes in v1:
time: 241 us
  blocking collectives  153 us (63%)
  waiting for transfers between devices  37.6 us (16%)
  starting transfers between devices  18.7 us (8%)
  between operations  13.5 us (6%)
  matrix products  7.96 us (3%)
  local copies, waits for them, and re-layouts  5.11 us (2%)
  other arithmetic  4.93 us (2%)
    all_gather x1, blocking collectives, body(): incoming_over = lax.all_gather(send_over, 'ad', tiled=True)  121 us
    all_to_all x1, blocking collectives, body(): lax.all_to_all(send_back, 'ad', split_axis=0, concat_axis=0, tiled=True)  32.5 us
    all_gather x1, waiting for transfers between devices, body(): down_sum = jnp.sum(lax.all_gather(down_part, 'tp'), axis=0)  29.5 us
    all_to_all x1, starting transfers between devices, body(): lax.all_to_all(send_rows, 'ad', split_axis=0, concat_axis=0, tiled=True)  18.6 us
    reduce_scatter x1, waiting for transfers between devices, body(): lax.psum_scatter(partial_base, 'tp', scatter_dimension=1, tiled=True)  7.39 us
  transfers between devices with their start and end apart: 3, of which 2 were waited for; matrix products, arithmetic and copies ran while one was open for 3% of the time, Pallas kernels for 0%

profile of v1, /device:TPU:2, one launch (start us, length us, event | category | flops | bytes accessed | tf_op | source)
XLA Modules:
  0.0 241.0 jit_solution(18104021679790323151)
XLA Ops:
  6.5 0.0 copy-start
  6.5 0.0 copy-start.2
  6.5 0.8 add_select_fusion.1
  7.4 0.1 fusion.11
  7.5 0.1 reduce_window_sum.11
  7.6 0.2 select_reduce_fusion
  7.8 0.7 add_select_fusion.2
  8.5 0.7 fusion.15
  9.2 0.1 broadcast_in_dim.19
  9.3 0.1 eq.83
  9.4 0.1 broadcast_in_dim.20
  9.5 1.3 convolution_convert_fusion
  10.8 1.0 reshape.112
  11.8 18.6 %all-to-all-start = ((bf16[64,4,1152]{2,1,0:T(4,128)(2,1)}), bf16[64,4,1152]{2,1,0:T(4,128)(2,1)S(1)}, u32[]{:S(2)}, u32[]{:S(2)}) async-start(bf16[64,4,1152]{2,1,0:T(4,128)(2,1)} %reshape.112), calls=%async_computation.1 | async-start | bytes 1179648 | tf_op jit(solution)/shard_map/all_to_all | solution.py:47
  30.4 0.0 all-gather.4.cloned.1.call-start
  30.5 0.1 select_n.32
  30.6 0.0 copy-done.2
  30.6 0.2 fusion
  30.7 120.6 %all-gather.1 = bf16[64,4,1152]{2,1,0:T(4,128)(2,1)S(1)} all-gather(bf16[1,4,1152]{2,1,0:T(4,128)(2,1)S(1)} %fusion), channel_id=1, replica_groups=mesh['ad'=64,'tp'=8] {'ad'}, dimensions={0}, use_global_device_ids=true | all-gather | bytes 599040 | tf_op jit(solution)/shard_map/all_gather | solution.py:46
  151.3 1.0 reshape.121
  152.3 0.0 copy-done
  152.3 0.0 copy-start.1
  152.3 2.5 %fusion.25 = f32[192,1024]{1,0:T(8,128)} fusion(bf16[192,1024]{1,0:T(8,128)(2,1)} %bitcast.29, bf16[1024,1024]{1,0:T(8,128)(2,1)S(1)} %copy-done), kind=kOutput, calls=%fused_computation.53 | convolution fusion | flops 402653184 | bytes 3276800 | tf_op jit(solution)/shard_map/dot_general | solution.py:48
  154.8 0.0 copy-done.1
  154.8 0.1 subtract_reduce_fusion
  154.9 0.0 all-to-all-done
  155.0 1.0 reshape.113
  155.9 0.9 convert_reduce_fusion
  156.9 1.7 fusion.4
  158.6 0.1 fusion.23
  158.6 0.7 multiply_reduce_fusion
  159.3 0.0 copy-start.3
  159.3 0.0 all-gather.4.cloned.1.call-update
  159.4 0.0 reduce-scatter.2.cloned.1.call-start
  159.4 0.7 reduce-scatter.2.cloned.1.call-update
  160.1 29.5 %all-gather.4.cloned.1.call-done = f32[4096,64]{0,1:T(8,128)} async-done(((f32[512,64]{0,1:T(8,128)}), f32[4096,64]{0,1:T(8,128)}) %all-gather.4.cloned.1.call-update) | async-done | bytes 1048592 | tf_op jit(solution)/shard_map/all_gather | solution.py:66
  189.7 1.8 copy.6
  191.5 0.3 bitcast_reduce_fusion
  191.8 0.0 copy-done.3
  191.8 0.3 fusion.1
  192.1 0.1 pad_maximum_fusion.5
  192.2 32.5 %all_to_all.10 = bf16[64,8,128]{2,1,0:T(8,128)(2,1)S(1)} all-to-all(bf16[64,8,128]{2,1,0:T(8,128)(2,1)S(1)} %pad_maximum_fusion.5), channel_id=1, replica_groups=mesh['ad'=64,'tp'=8] {'ad'}, dimensions={0} | all-to-all | bytes 262144 | tf_op jit(solution)/shard_map/all_to_all | solution.py:78
  224.7 0.1 convert_reduce_fusion.1
  224.8 0.2 fusion.12
  225.0 7.4 %reduce-scatter.2.cloned.1.call-done = f32[192,128]{1,0:T(8,128)} async-done(((f32[192,1024]{1,0:T(8,128)}), f32[192,128]{1,0:T(8,128)}) %reduce-scatter.2.cloned.1.call-update) | async-done | bytes 98320 | tf_op jit(solution)/shard_map/reduce_scatter | solution.py:50
  232.4 1.8 fusion.3
  (4 shorter events, 0.0 us)
Async XLA Ops:
  6.5 145.8 %copy-start = (bf16[1024,1024]{1,0:T(8,128)(2,1)S(1)}, bf16[1024,1024]{1,0:T(8,128)(2,1)}, u32[]{:S(2)}) copy-start(bf16[1024,1024]{1,0:T(8,128)(2,1)} %param.7) | copy-start | bytes 6291460
  6.5 24.0 %copy-start.2 = (bf16[4,48,1024]{2,1,0:T(8,128)(2,1)S(1)}, bf16[4,48,1024]{2,1,0:T(8,128)(2,1)}, u32[]{:S(2)}) copy-start(bf16[4,48,1024]{2,1,0:T(8,128)(2,1)} %param.5) | copy-start | bytes 1179652
  11.8 143.2 %all-to-all-start = ((bf16[64,4,1152]{2,1,0:T(4,128)(2,1)}), bf16[64,4,1152]{2,1,0:T(4,128)(2,1)S(1)}, u32[]{:S(2)}, u32[]{:S(2)}) async-start(bf16[64,4,1152]{2,1,0:T(4,128)(2,1)} %reshape.112), calls=%async_computation.1 | async-start | bytes 1179648 | tf_op jit(solution)/shard_map/all_to_all | solution.py:47
  30.4 159.2 %all-gather.4.cloned.1.call-start = ((), (), s32[]{:S(2)}) async-start(), calls=%async_computation.4 | async-start | bytes 1179648 | tf_op jit(solution)/shard_map/all_gather | solution.py:66
  152.3 2.5 %copy-start.1 = (bf16[256,1152]{1,0:T(8,128)(2,1)S(1)}, bf16[256,1152]{1,0:T(8,128)(2,1)}, u32[]{:S(2)}) copy-start(bf16[256,1152]{1,0:T(8,128)(2,1)} %reshape.121) | copy-start | bytes 1769476
  159.3 32.4 %copy-start.3 = (bf16[4,64,128]{2,1,0:T(8,128)(2,1)S(1)}, bf16[4,64,128]{2,1,0:T(8,128)(2,1)}, u32[]{:S(2)}) copy-start(bf16[4,64,128]{2,1,0:T(8,128)(2,1)} %param.9) | copy-start | bytes 196612
  159.4 73.0 %reduce-scatter.2.cloned.1.call-start = ((), (), s32[]{:S(2)}) async-start(), calls=%async_computation.3 | async-start | bytes 884736 | tf_op jit(solution)/shard_map/reduce_scatter | solution.py:50
Sparse Core Ops, SparseCore 0:
  159.5 30.1 all-gather.3
  192.5 39.8 reduce-scatter.1

commit v2 on v0

--- a/solution.py
+++ b/solution.py
@@ -43,7 +43,9 @@
     send_over = jnp.dot(dispatch_over, rows_tagged, preferred_element_type=jnp.float32).astype(
         jnp.bfloat16
     )
-    incoming_over = lax.all_gather(send_over, "ad", tiled=True)
+    incoming_over = jnp.concatenate(
+        lax.all_to_all(jnp.stack([send_over] * lax.axis_size("ad")), "ad", 0, 0), axis=0
+    )
     incoming = lax.all_to_all(send_rows, "ad", split_axis=0, concat_axis=0, tiled=True)
     partial_base = jnp.dot(gathered_rows, key_base_weight, preferred_element_type=jnp.float32)
     partial_base, incoming_over = lax.optimization_barrier((partial_base, incoming_over))

time: 222 us -> 167 us (0.75)
  blocking collectives: 174 us -> 47.3 us
  waiting for transfers between devices: 0.03 us -> 64.3 us
  starting transfers between devices: 18.7 us -> 24.6 us
    all_gather x1 -> x0, blocking collectives: 121 us -> none  [body(): incoming_over = lax.all_gather(send_over, 'ad', tiled=True)]
    all_to_all x0 -> x1, waiting for transfers between devices: none -> 33.1 us  [body(): lax.all_to_all(jnp.stack([send_over] * lax.axis_size('ad')), 'ad', 0, 0)]
    all_to_all x1, waiting for transfers between devices: 0.01 us -> 31.1 us  [body(): lax.all_to_all(send_rows, 'ad', split_axis=0, concat_axis=0, tiled=True)]
    all_to_all x0 -> x1, starting transfers between devices: none -> 18.6 us  [body(): lax.all_to_all(jnp.stack([send_over] * lax.axis_size('ad')), 'ad', 0, 0)]
    all_to_all x1, starting transfers between devices: 18.6 us -> 5.95 us  [body(): lax.all_to_all(send_rows, 'ad', split_axis=0, concat_axis=0, tiled=True)]
    all_to_all x1, blocking collectives: 28.5 us -> 22.5 us  [body(): lax.all_to_all(send_back, 'ad', split_axis=0, concat_axis=0, tiled=True)]
  transfers between devices with their start and end apart: 2 -> 3, of which waited for: 0 -> 2; matrix products, arithmetic and copies ran while one was open for 4% -> 6% of each run, Pallas kernels for 0% -> 0%
where the time goes in v2:
time: 167 us; the launch traced here: 166 us
  waiting for transfers between devices  64.3 us (39%)
  blocking collectives  47.3 us (28%)
  starting transfers between devices  24.6 us (15%)
  between operations  13.5 us (8%)
  matrix products  8.89 us (5%)
  other arithmetic  4.01 us (2%)
  local copies, waits for them, and re-layouts  3.43 us (2%)
    all_to_all x1, waiting for transfers between devices, body(): lax.all_to_all(jnp.stack([send_over] * lax.axis_size('ad')), 'ad', 0, 0)  33.1 us
    all_to_all x1, waiting for transfers between devices, body(): lax.all_to_all(send_rows, 'ad', split_axis=0, concat_axis=0, tiled=True)  31.1 us
    psum x1, blocking collectives, body(): down_sum = lax.psum(down_part, 'tp')  24.9 us
    all_to_all x1, blocking collectives, body(): lax.all_to_all(send_back, 'ad', split_axis=0, concat_axis=0, tiled=True)  22.5 us
    all_to_all x1, starting transfers between devices, body(): lax.all_to_all(jnp.stack([send_over] * lax.axis_size('ad')), 'ad', 0, 0)  18.6 us
    all_to_all x1, starting transfers between devices, body(): lax.all_to_all(send_rows, 'ad', split_axis=0, concat_axis=0, tiled=True)  5.95 us
  transfers between devices with their start and end apart: 3, of which 2 were waited for; matrix products, arithmetic and copies ran while one was open for 6% of the time, Pallas kernels for 0%

profile of v2, /device:TPU:2, one launch (start us, length us, event | category | flops | bytes accessed | tf_op | source)
XLA Modules:
  0.0 166.1 jit_solution(11033693430884651265)
XLA Ops:
  6.5 0.0 copy-start
  6.5 0.8 add_select_fusion.1
  7.4 0.1 fusion.10
  7.5 0.1 reduce_window_sum.11
  7.6 0.2 select_reduce_fusion
  7.8 0.7 add_select_fusion.2
  8.5 0.7 fusion.14
  9.2 0.1 broadcast_in_dim.19
  9.3 0.1 select_n.32
  9.4 0.1 broadcast_in_dim.20
  9.5 1.2 convolution_convert_fusion.1
  10.6 1.0 stack.2
  11.6 18.6 %all-to-all-start = ((bf16[64,4,1152]{2,1,0:T(4,128)(2,1)}), bf16[64,4,1152]{2,1,0:T(4,128)(2,1)S(1)}, u32[]{:S(2)}, u32[]{:S(2)}) async-start(bf16[64,4,1152]{2,1,0:T(4,128)(2,1)} %stack.2), calls=%async_computation | async-start | bytes 1179648 | tf_op jit(solution)/shard_map/all_to_all | solution.py:47
  30.3 0.1 eq.83
  30.4 1.3 convolution_convert_fusion
  31.7 1.0 reshape.116
  32.7 33.1 %all-to-all-done = bf16[64,4,1152]{2,1,0:T(4,128)(2,1)S(1)} async-done(((bf16[64,4,1152]{2,1,0:T(4,128)(2,1)}), bf16[64,4,1152]{2,1,0:T(4,128)(2,1)S(1)}, u32[]{:S(2)}, u32[]{:S(2)}) %all-to-all-start) | async-done | bytes 589856 | tf_op jit(solution)/shard_map/all_to_all | solution.py:47
  65.8 5.9 %all-to-all-start.1 = ((bf16[64,4,1152]{2,1,0:T(4,128)(2,1)}), bf16[64,4,1152]{2,1,0:T(4,128)(2,1)S(1)}, u32[]{:S(2)}, u32[]{:S(2)}) async-start(bf16[64,4,1152]{2,1,0:T(4,128)(2,1)} %reshape.116), calls=%async_computation.2 | async-start | bytes 1179648 | tf_op jit(solution)/shard_map/all_to_all | solution.py:49
  71.7 0.0 reduce-scatter.2.cloned.1.call-start
  71.8 0.0 copy-done
  71.8 2.5 %fusion.24 = f32[192,1024]{1,0:T(8,128)} fusion(bf16[192,1024]{1,0:T(8,128)(2,1)} %bitcast.22, bf16[1024,1024]{1,0:T(8,128)(2,1)S(1)} %copy-done), kind=kOutput, calls=%fused_computation.51 | convolution fusion | flops 402653184 | bytes 3276800 | tf_op jit(solution)/shard_map/dot_general | solution.py:50
  74.3 1.0 reshape.115
  75.2 0.0 reduce-scatter.2.cloned.1.call-update
  75.3 31.1 %all-to-all-done.1 = bf16[64,4,1152]{2,1,0:T(4,128)(2,1)S(1)} async-done(((bf16[64,4,1152]{2,1,0:T(4,128)(2,1)}), bf16[64,4,1152]{2,1,0:T(4,128)(2,1)S(1)}, u32[]{:S(2)}, u32[]{:S(2)}) %all-to-all-start.1) | async-done | bytes 589856 | tf_op jit(solution)/shard_map/all_to_all | solution.py:49
  106.4 0.1 reshape.117
  106.5 0.0 copy-start.1
  106.5 0.1 convert_reduce_fusion
  106.7 1.7 %fusion.3 = f32[512,256]{0,1:S(1)} fusion(bf16[1024,256]{0,1:T(8,128)(2,1)} %bitcast.26, bf16[256,1152]{1,0:T(8,128)(2,1)} %reshape.115, bf16[256,1152]{1,0:T(8,128)(2,1)S(1)} %reshape.117), kind=kOutput, calls=%fused_computation.8 | convolution fusion | flops 270532608 | bytes 2228224
  108.3 1.0 subtract_reduce_fusion
  109.3 0.1 fusion.22
  109.4 0.1 multiply_reduce_fusion
  109.4 24.9 %all-reduce.1 = bf16[512,64]{0,1:T(8,128)(2,1)S(1)} all-reduce(f32[512,64]{0,1:T(8,128)S(1)} %multiply_reduce_fusion), channel_id=1, replica_groups=mesh['ad'=64,'tp'=8] {'tp'}, use_global_device_ids=true, to_apply=%region_4.5 | all-reduce | flops 32768 | bytes 196608 | tf_op jit(solution)/shard_map/psum | solution.py:68
  134.3 0.0 copy-done.1
  134.3 0.3 fusion
  134.6 0.1 pad_maximum_fusion.5
  134.7 22.5 %all_to_all.15 = bf16[64,8,128]{2,1,0:T(8,128)(2,1)S(1)} all-to-all(bf16[64,8,128]{2,1,0:T(8,128)(2,1)S(1)} %pad_maximum_fusion.5), channel_id=1, replica_groups=mesh['ad'=64,'tp'=8] {'ad'}, dimensions={0} | all-to-all | bytes 262144 | tf_op jit(solution)/shard_map/all_to_all | solution.py:80
  157.2 0.1 convert_reduce_fusion.1
  157.3 0.2 fusion.11
  157.5 0.0 reduce-scatter.2.cloned.1.call-done
  157.5 1.8 %fusion.2 = bf16[192,128]{1,0:T(8,128)(2,1)} fusion(f32[192,128]{1,0:T(8,128)} %reduce-scatter.2.cloned.1.call-done, f32[192,128]{1,0:T(8,128)S(1)} %fusion.11, bf16[256,128]{1,0:T(8,128)(2,1)S(1)} %bitcast.23, s32[192]{0:T(256)S(1)} %eq.83), kind=kOutput, calls=%fused_computation.6 | convolution fusion | flops 12705792 | bytes 312064 | tf_op jit(solution)/shard_map/dot_general | solution.py:83
  (4 shorter events, 0.0 us)
Async XLA Ops:
  6.5 65.3 %copy-start = (bf16[1024,1024]{1,0:T(8,128)(2,1)S(1)}, bf16[1024,1024]{1,0:T(8,128)(2,1)}, u32[]{:S(2)}) copy-start(bf16[1024,1024]{1,0:T(8,128)(2,1)} %param.7) | copy-start | bytes 6291460
  11.6 54.2 %all-to-all-start = ((bf16[64,4,1152]{2,1,0:T(4,128)(2,1)}), bf16[64,4,1152]{2,1,0:T(4,128)(2,1)S(1)}, u32[]{:S(2)}, u32[]{:S(2)}) async-start(bf16[64,4,1152]{2,1,0:T(4,128)(2,1)} %stack.2), calls=%async_computation | async-start | bytes 1179648 | tf_op jit(solution)/shard_map/all_to_all | solution.py:47
  65.8 40.6 %all-to-all-start.1 = ((bf16[64,4,1152]{2,1,0:T(4,128)(2,1)}), bf16[64,4,1152]{2,1,0:T(4,128)(2,1)S(1)}, u32[]{:S(2)}, u32[]{:S(2)}) async-start(bf16[64,4,1152]{2,1,0:T(4,128)(2,1)} %reshape.116), calls=%async_computation.2 | async-start | bytes 1179648 | tf_op jit(solution)/shard_map/all_to_all | solution.py:49
  71.7 85.8 %reduce-scatter.2.cloned.1.call-start = ((), (), s32[]{:S(2)}) async-start(), calls=%async_computation.4 | async-start | bytes 884736 | tf_op jit(solution)/shard_map/reduce_scatter | solution.py:52
  106.5 27.8 %copy-start.1 = (bf16[4,64,128]{2,1,0:T(8,128)(2,1)S(1)}, bf16[4,64,128]{2,1,0:T(8,128)(2,1)}, u32[]{:S(2)}) copy-start(bf16[4,64,128]{2,1,0:T(8,128)(2,1)} %param.9) | copy-start | bytes 196612
Sparse Core Ops, SparseCore 0:
  75.4 40.6 reduce-scatter.1
